TPU v7x, 256 devices: a whole 4x4x8 slice. The times are simulated.
256 devices in a mesh: ctx: 8 (over z_lo, core), ep: 32 (over y, x, z_hi).
Axes of the slice: x: 4, y: 4, z: 8 (z_hi: 2, z_lo: 4; z = z_hi * 4 + z_lo), core: 2. Of those that a mesh axis runs over, the one named last changes fastest.
Arguments:
- queries: bfloat16 [32768, 2048], P(('ctx', 'ep')), may hold values from -40 to 40
- keys: bfloat16 [32768, 256], P(('ctx', 'ep')), may hold values from -40 to 40
- values: bfloat16 [32768, 256], P(('ctx', 'ep')), may hold values from -6 to 6
- prior_out: bfloat16 [32768, 2048], P(('ctx', 'ep')), may hold values from -6 to 6
- prior_lse: float32 [32768, 16], P(('ctx', 'ep')), may hold values from 4 to 8
- residual: bfloat16 [32768, 2048], P(('ctx', 'ep')), may hold values from -40 to 40
- out_proj: bfloat16 [2048, 2048], P(('ctx', 'ep')), may hold values from -0.5 to 0.5
- norm_gain: float32 [2048], replicated, may hold values from 0.5 to 1.5
- expert_in: bfloat16 [32, 2048, 1536], P('ep'), may hold values from -0.125 to 0.125
- expert_out: bfloat16 [32, 768, 2048], P('ep'), may hold values from -0.21875 to 0.21875
- expert_ids: int32 [32768, 8], P(('ctx', 'ep')), may hold values from 0 to 31, as said below
- route_weight: float32 [32768, 8], P(('ctx', 'ep')), may hold values from 0.05 to 0.6
Outputs:
- layer_out: bfloat16 [32768, 2048], P(('ctx', 'ep'))
- attended: bfloat16 [32768, 2048], P(('ctx', 'ep'))
Inputs may be any that keep to these rules, and one draw needn't show every extreme that they name: `expert_ids`: each row names 8 different experts. In the rows of one device no expert is named more than 40 times, and one expert is named exactly 40 times in the rows of every device.
All inputs are finite; a program needn't handle non-finite values.
Results may differ from a plain program's by a relative error of at most 0.0061.
Values may be sent and summed in bfloat16 or wider, within the bound.
A program may use at most 128 MiB of HBM per device.

v0:
```python
import math
import jax
import jax.numpy as jnp
from jax import lax
from jax.sharding import PartitionSpec as P

HEADS = 16
KVH = 2
HD = 128
GROUP = 8


def passed_along(shard, axis, by):
    devices = lax.axis_size(axis)
    return lax.ppermute(shard, axis, [(i, (i + by) % devices) for i in range(devices)])


def run_expert(inputs, weight_in, weight_out, hidden_units):
    flat_in = inputs.reshape(-1, inputs.shape[-1])
    gate_up = jnp.dot(flat_in, weight_in, preferred_element_type=jnp.float32)
    activated = (jax.nn.silu(gate_up[:, :hidden_units]) * gate_up[:, hidden_units:]).astype(
        jnp.bfloat16
    )
    replies = jnp.dot(activated, weight_out, preferred_element_type=jnp.float32).astype(
        jnp.bfloat16
    )
    return replies.reshape(inputs.shape[:-1] + (weight_out.shape[-1],))


def shards(
    queries,
    keys,
    values,
    prior_out,
    prior_lse,
    residual,
    out_proj,
    norm_gain,
    expert_in,
    expert_out,
    expert_ids,
    route_weight,
):
    local_rows = queries.shape[0]
    ctx_count = lax.axis_size("ctx")
    ctx_here = lax.axis_index("ctx")
    ep_count = lax.axis_size("ep")
    reach_steps = min(2, ctx_count - 1)
    kv_pair = jnp.stack([keys, values])
    arrived = []
    current = kv_pair
    for stride in range(reach_steps):
        current = passed_along(current, "ctx", 1)
        arrived.append(current)
    window = jnp.concatenate(arrived, axis=1)
    width_kv = window.shape[1]
    key_win = window[0].reshape(width_kv, KVH, HD)
    value_win = window[1].reshape(width_kv, KVH, HD)
    query_blk = queries.reshape(local_rows, KVH, GROUP, HD)
    scores = jnp.einsum(
        "ighd,jgd->ghij", query_blk, key_win, preferred_element_type=jnp.float32
    ) / math.sqrt(HD)
    positions = jnp.arange(width_kv, dtype=jnp.int32)
    key_local = positions % local_rows
    key_ctx = (ctx_here - (positions // local_rows + 1)) % ctx_count
    query_local = jnp.arange(local_rows, dtype=jnp.int32)[:, None]
    visible = (key_local[None, :] < query_local) | (key_local[None, :] == query_local) & (
        key_ctx[None, :] <= ctx_here
    )
    scores = jnp.where(visible, scores, -jnp.inf)
    lse_prior = prior_lse.reshape(local_rows, KVH, GROUP).transpose(1, 2, 0)
    top_score = jnp.maximum(lse_prior, jnp.max(scores, axis=-1))
    weights = jnp.exp(scores - top_score[..., None])
    prior_weight = jnp.exp(lse_prior - top_score)
    totals = prior_weight + jnp.sum(weights, axis=-1)
    gathered = jnp.einsum(
        "ghij,jgd->ighd",
        weights.astype(jnp.bfloat16),
        value_win,
        preferred_element_type=jnp.float32,
    )
    prior_part = (
        prior_out.reshape(local_rows, KVH, GROUP, HD).astype(jnp.float32)
        * prior_weight.transpose(2, 0, 1)[..., None]
    )
    attended = ((prior_part + gathered) / totals.transpose(2, 0, 1)[..., None]).astype(jnp.bfloat16)
    attended = attended.reshape(local_rows, HEADS * HD)
    model_width = out_proj.shape[1]
    column_half = model_width // 2
    core = ctx_here % 2
    column_rows = lax.all_gather(out_proj, "ctx", axis=0, tiled=True)
    own_half = lax.dynamic_slice_in_dim(column_rows, core * column_half, column_half, axis=1)
    own_half = lax.all_gather(own_half, "ep", axis=0, tiled=True)
    other_half = lax.ppermute(own_half, "ctx", [(i, i ^ 1) for i in range(ctx_count)])
    block_rows = out_proj.shape[0]
    attended_perm = (
        attended.reshape(local_rows, ctx_count, ep_count, block_rows)
        .transpose(0, 2, 1, 3)
        .reshape(local_rows, HEADS * HD)
    )
    own_part = jnp.dot(attended_perm, own_half, preferred_element_type=jnp.float32)
    other_part = jnp.dot(attended_perm, other_half, preferred_element_type=jnp.float32)
    projected = jnp.zeros((local_rows, model_width), jnp.float32)
    projected = lax.dynamic_update_slice_in_dim(projected, own_part, core * column_half, axis=1)
    projected = lax.dynamic_update_slice_in_dim(
        projected, other_part, (1 - core) * column_half, axis=1
    )
    mixed_state = (residual.astype(jnp.float32) + projected).astype(jnp.bfloat16)
    state_f = lax.optimization_barrier(mixed_state).astype(jnp.float32)
    normed = (
        state_f * lax.rsqrt(jnp.mean(state_f * state_f, axis=-1, keepdims=True) + 1e-06) * norm_gain
    ).astype(jnp.bfloat16)
    experts_all = ep_count * expert_in.shape[0]
    top_count = expert_ids.shape[1]
    capacity = max(
        local_rows // 4, top_count * ((local_rows + experts_all - 2) // (experts_all - 1))
    )
    flat_ids = expert_ids.reshape(-1)
    one_hot = (flat_ids[:, None] == jnp.arange(experts_all, dtype=jnp.int32)[None, :]).astype(
        jnp.int32
    )
    earlier = jnp.cumsum(one_hot, axis=0) - one_hot
    slot_ids = flat_ids * capacity + jnp.sum(earlier * one_hot, axis=1)
    outgoing = jnp.zeros((experts_all * capacity, model_width), jnp.bfloat16)
    outgoing = (
        outgoing.at[slot_ids]
        .set(jnp.repeat(normed, top_count, axis=0))
        .reshape(experts_all, capacity, model_width)
    )
    weight_in = expert_in[0]
    weight_out = expert_out[0]
    hidden_units = weight_out.shape[0]
    replies = run_expert(
        lax.all_to_all(outgoing, "ep", split_axis=0, concat_axis=0, tiled=True),
        weight_in,
        weight_out,
        hidden_units,
    )
    returned = lax.all_to_all(replies, "ep", split_axis=0, concat_axis=0, tiled=True)
    picked = returned.reshape(experts_all * capacity, model_width)[slot_ids].reshape(
        local_rows, top_count, model_width
    )
    combined = jnp.sum(route_weight[:, :, None] * picked.astype(jnp.float32), axis=1)
    layer_out = (state_f + combined).astype(jnp.bfloat16)
    return (layer_out, attended)


def solution(mesh):
    return jax.shard_map(
        shards,
        mesh=mesh,
        in_specs=(
            P(("ctx", "ep"), None),
            P(("ctx", "ep"), None),
            P(("ctx", "ep"), None),
            P(("ctx", "ep"), None),
            P(("ctx", "ep"), None),
            P(("ctx", "ep"), None),
            P(("ctx", "ep"), None),
            P(),
            P("ep", None, None),
            P("ep", None, None),
            P(("ctx", "ep"), None),
            P(("ctx", "ep"), None),
        ),
        out_specs=(P(("ctx", "ep"), None), P(("ctx", "ep"), None)),
        check_vma=False,
    )
```

profile of v0, /device:TPU:94, one launch (start us, length us, event | category | flops | bytes accessed | tf_op | source)
XLA Modules:
  0.0 471.1 jit_solution(506274494953376835)
XLA Ops:
  7.2 0.0 copy-start
  7.2 0.0 all-gather.2.cloned.1.call-start
  7.2 12.8 %all_gather.6 = bf16[64,2048]{1,0:T(8,128)(2,1)S(1)} all-gather(bf16[8,2048]{1,0:T(8,128)(2,1)} %param.18), channel_id=1, replica_groups=mesh['ctx'=8,'ep'=32] {'ctx'}, dimensions={0}, use_global_device_ids=true | all-gather | bytes 294912 | tf_op jit(solution)/shard_map/all_gather | solution.py:91
  20.1 0.7 constant_dynamic-slice_fusion
  20.7 0.0 all-gather.2.cloned.1.call-update
  20.8 111.6 %all-gather.2.cloned.1.call-done = bf16[2048,1024]{1,0:T(8,128)(2,1)} async-done(((bf16[64,1024]{1,0:T(8,128)(2,1)}), bf16[2048,1024]{1,0:T(8,128)(2,1)}) %all-gather.2.cloned.1.call-update) | async-done | bytes 4194320 | tf_op jit(solution)/shard_map/all_gather | solution.py:93
  132.4 0.0 collective-permute-start.2
  132.4 0.9 copy.21
  133.3 1.0 copy.22
  134.3 0.0 copy-start.7
  134.3 0.7 pad_maximum_fusion
  135.0 0.5 collective-permute-start
  135.5 0.8 copy.29
  136.3 0.1 eq.44
  136.4 9.0 %reduce-window.6 = s32[32,8,128]{2,1,0:T(8,128)S(1)} reduce-window(s32[32,8,128]{2,1,0:T(8,128)S(1)} %fusion.28, s32[]{:T(128)} %constant.73.clone.1), window={size=1x1x128 pad=0_0x0_0x127_0}, to_apply=%region_2.3 | reduce-window | flops 4161536 | bytes 262148 | tf_op jit(solution)/shard_map/reduce-window
  145.4 0.1 slice.28
  145.5 0.1 copy.31
  145.7 0.1 copy.32
  145.8 0.1 fusion.26
  145.9 0.1 broadcast_add_fusion
  146.0 0.7 broadcast_multiply_fusion
  146.7 0.1 eq.40
  146.8 0.1 copy.28
  146.9 0.1 mul.75
  147.1 0.0 collective-permute-done
  147.1 0.1 collective-permute-start.1
  147.2 2.0 copy.39
  149.1 2.3 copy.20
  151.5 1.0 constant_dynamic-update-slice_fusion.1
  152.5 0.0 collective-permute-done.1
  152.5 1.6 fusion.38
  154.1 0.0 copy-done.7
  154.1 0.3 fusion.11
  154.5 0.0 copy-start.3
  154.5 0.0 copy-done.5
  154.5 0.5 fusion.15
  155.0 0.0 copy-start.4
  155.0 0.1 copy.26
  155.2 0.7 copy-done.4
  155.9 0.1 broadcast_in_dim.14
  156.0 0.9 copy-done.3
  156.8 0.7 convolution_dynamic-update-slice_fusion.1
  157.6 0.0 copy-start.8
  157.6 0.0 collective-permute-done.2
  157.6 3.0 convolution_dynamic-update-slice_fusion
  160.6 0.0 copy-done.6
  160.6 0.1 add_convert_fusion
  160.7 0.0 copy-start.1
  160.7 0.2 fusion.16
  160.9 0.6 copy-done.1
  161.5 0.0 copy-done.8
  161.5 1.0 fusion.18
  162.5 10.1 %scatter_custom_fusion = bf16[1280,2048]{1,0:T(8,128)(2,1)} fusion(s32[1024]{0:T(1024)S(1)} %bitcast.102, bf16[]{:T(256)} %constant.86.clone.1, bf16[128,2048]{1,0:T(8,128)(2,1)} %fusion.18), kind=kCustom, calls=%fused_computation.7 | custom fusion | bytes 5767170 | tf_op jit(solution)/shard_map/scatter | solution.py:127
  172.5 127.9 %all_to_all.10 = bf16[32,40,2048]{2,1,0:T(8,128)(2,1)S(1)} all-to-all(bf16[32,40,2048]{2,1,0:T(8,128)(2,1)} %bitcast.85), channel_id=1, replica_groups=mesh['ctx'=8,'ep'=32] {'ep'}, dimensions={0} | all-to-all | bytes 10485760 | tf_op jit(solution)/shard_map/all_to_all | solution.py:134
  300.4 10.5 %fusion.1 = f32[1280,1536]{1,0:T(8,128)S(1)} fusion(bf16[1280,2048]{1,0:T(8,128)(2,1)S(1)} %bitcast.87, bf16[1,2048,1536]{2,1,0:T(8,128)(2,1)} %param.20), kind=kOutput, calls=%fused_computation.5 | convolution fusion | flops 8053063680 | bytes 19398656 | tf_op jit(solution)/shard_map/dot_general | solution.py:20
  311.0 6.1 %convolution_convert_fusion = bf16[1280,2048]{1,0:T(8,128)(2,1)} fusion(bf16[1,768,2048]{2,1,0:T(8,128)(2,1)S(1)} %copy-done, f32[1280,1536]{1,0:T(8,128)S(1)} %fusion.1), kind=kOutput, calls=%fused_computation.4 | convolution fusion | flops 4035051520 | bytes 16252928 | tf_op jit(solution)/shard_map/dot_general | solution.py:24
  317.1 8.9 %all-to-all-start.1 = ((bf16[32,40,2048]{2,1,0:T(8,128)(2,1)}), bf16[32,40,2048]{2,1,0:T(8,128)(2,1)}, u32[]{:S(2)}, u32[]{:S(2)}) async-start(bf16[32,40,2048]{2,1,0:T(8,128)(2,1)} %bitcast.86), calls=%async_computation.1 | async-start | bytes 10485760 | tf_op jit(solution)/shard_map/all_to_all | solution.py:139
  325.9 0.1 copy.27
  326.0 2.0 copy.33
  328.1 116.6 %all-to-all-done.1 = bf16[32,40,2048]{2,1,0:T(8,128)(2,1)} async-done(((bf16[32,40,2048]{2,1,0:T(8,128)(2,1)}), bf16[32,40,2048]{2,1,0:T(8,128)(2,1)}, u32[]{:S(2)}, u32[]{:S(2)}) %all-to-all-start.1) | async-done | bytes 5242912 | tf_op jit(solution)/shard_map/all_to_all | solution.py:139
  444.7 12.0 %gather_fusion = bf16[1024,2048]{1,0:T(8,128)(2,1)} fusion(bf16[1280,2048]{1,0:T(8,128)(2,1)} %bitcast.28, s32[1024]{0:T(1024)S(1)} %broadcast_clamp_fusion), kind=kCustom, calls=%fused_computation | custom fusion | bytes 8392704 | tf_op jit(solution)/shard_map/gather | solution.py:140
  456.7 6.6 %fusion = f32[128,2048]{1,0:T(8,128)S(1)} fusion(bf16[1024,2048]{1,0:T(8,128)(2,1)} %gather_fusion, f32[128,8]{1,0:T(8,128)S(1)} %copy.27), kind=kLoop, calls=%fused_computation.3 | loop fusion | flops 6029312 | bytes 5246976 | tf_op jit(solution)/shard_map/reduce_sum | solution.py:143
  463.3 0.0 copy-done.2
  463.3 0.9 fusion.19
  (19 shorter events, 0.2 us)
Async XLA Ops:
  7.2 303.8 %copy-start = (bf16[1,768,2048]{2,1,0:T(8,128)(2,1)S(1)}, bf16[1,768,2048]{2,1,0:T(8,128)(2,1)}, u32[]{:S(2)}) copy-start(bf16[1,768,2048]{2,1,0:T(8,128)(2,1)} %param.21) | copy-start | bytes 9437188
  7.2 125.2 %all-gather.2.cloned.1.call-start = ((), (), s32[]{:S(2)}) async-start(), calls=%async_computation.2 | async-start | bytes 4325376 | tf_op jit(solution)/shard_map/all_gather | solution.py:93
  132.4 25.2 %collective-permute-start.2 = (bf16[2048,1024]{1,0:T(8,128)(2,1)}, bf16[2048,1024]{1,0:T(8,128)(2,1)}, u32[]{:S(2)}, u32[]{:S(2)}) collective-permute-start(bf16[2048,1024]{1,0:T(8,128)(2,1)} %all-gather.2.cloned.1.call-done), channel_id=1, source_target_pairs={{0,32},{32,0},{64,96},{96,64},{128,160},{160,128},{192,224},{224,1... | collective-permute-start | bytes 12582920 | tf_op jit(solution)/shard_map/ppermute | solution.py:94
  134.3 19.8 %copy-start.7 = (f32[128,16]{0,1:T(8,128)S(1)}, f32[128,16]{0,1:T(8,128)}, u32[]{:S(2)}) copy-start(f32[128,16]{0,1:T(8,128)} %param.16) | copy-start | bytes 24580
  135.0 12.1 %collective-permute-start = (bf16[2,128,256]{1,2,0:T(8,128)(2,1)}, bf16[2,128,256]{1,2,0:T(8,128)(2,1)}, u32[]{:S(2)}, u32[]{:S(2)}) collective-permute-start(bf16[2,128,256]{1,2,0:T(8,128)(2,1)} %pad_maximum_fusion), channel_id=1, source_target_pairs={{0,32},{32,64},{64,96},{96,128},{128,160},{160,192},{192,224},{224... | collective-permute-start | bytes 393224 | tf_op jit(solution)/shard_map/ppermute | solution.py:15
  147.1 5.4 %collective-permute-start.1 = (bf16[2,128,256]{1,2,0:T(8,128)(2,1)}, bf16[2,128,256]{1,2,0:T(8,128)(2,1)S(1)}, u32[]{:S(2)}, u32[]{:S(2)}) collective-permute-start(bf16[2,128,256]{1,2,0:T(8,128)(2,1)} %collective-permute-done), channel_id=1, source_target_pairs={{0,32},{32,64},{64,96},{96,128},{128,160},{160,192},{192,224},{224... | collective-permute-start | bytes 393224 | tf_op jit(solution)/shard_map/ppermute | solution.py:15
  151.4 3.0 copy-start.5
  154.5 2.4 copy-start.3
  155.0 0.8 copy-start.4
  156.8 3.7 copy-start.6
  157.6 3.9 copy-start.8
  160.7 0.8 copy-start.1
  317.1 8.9 %copy-start.9 = (f32[128,8]{0,1:T(8,128)S(1)}, f32[128,8]{0,1:T(8,128)}, u32[]{:S(2)}) copy-start(f32[128,8]{0,1:T(8,128)} %param.23) | copy-start | bytes 12292
  317.1 127.6 %all-to-all-start.1 = ((bf16[32,40,2048]{2,1,0:T(8,128)(2,1)}), bf16[32,40,2048]{2,1,0:T(8,128)(2,1)}, u32[]{:S(2)}, u32[]{:S(2)}) async-start(bf16[32,40,2048]{2,1,0:T(8,128)(2,1)} %bitcast.86), calls=%async_computation.1 | async-start | bytes 10485760 | tf_op jit(solution)/shard_map/all_to_all | solution.py:139
  456.7 6.6 %copy-start.2 = (bf16[128,2048]{1,0:T(8,128)(2,1)S(1)}, bf16[128,2048]{1,0:T(8,128)(2,1)}, u32[]{:S(2)}) copy-start(bf16[128,2048]{1,0:T(8,128)(2,1)} %copy-done.1) | copy-start | bytes 1572868
Sparse Core Ops, SparseCore 0:
  20.9 111.4 all-gather.1
where the time goes:
time: 472 us; the launch traced here: 471 us
  waiting for transfers between devices  228 us (48%)
  blocking collectives  141 us (30%)
  local copies, waits for them, and re-layouts  36 us (8%)
  matrix products  22.4 us (5%)
  other arithmetic  19.8 us (4%)
  between operations  14.4 us (3%)
  starting transfers between devices  9.49 us (2%)
    all_to_all x1, blocking collectives, shards(): lax.all_to_all(outgoing, 'ep', split_axis=0, concat_axis=0, tiled=True)  128 us
    all_to_all x1, waiting for transfers between devices, shards(): lax.all_to_all(replies, 'ep', split_axis=0, concat_axis=0, tiled=True)  117 us
    all_gather x1, waiting for transfers between devices, shards(): own_half = lax.all_gather(own_half, 'ep', axis=0, tiled=True)  112 us
    all_gather x1, blocking collectives, shards(): column_rows = lax.all_gather(out_proj, 'ctx', axis=0, tiled=True)  12.8 us
    gather x1, local copies, waits for them, and re-layouts, shards(): returned.reshape(experts_all * capacity, model_width)[slot_ids]  12 us
    dot_general x1, matrix products, run_expert(): gate_up = jnp.dot(flat_in, weight_in, preferred_element_type=jnp.float32)  10.5 us
    scatter x1, local copies, waits for them, and re-layouts, shards(): outgoing = outgoing.at[slot_ids].set(jnp.repeat(normed, top_count, axis=0...  10.1 us
    unnamed x27, local copies, waits for them, and re-layouts  9.98 us
  transfers between devices with their start and end apart: 5, of which 2 were waited for; matrix products, arithmetic and copies ran while one was open for 5% of the time, Pallas kernels for 0%

commit v1 on v0

--- a/solution.py
+++ b/solution.py
@@ -90,7 +90,9 @@
     core = ctx_here % 2
     column_rows = lax.all_gather(out_proj, "ctx", axis=0, tiled=True)
     own_half = lax.dynamic_slice_in_dim(column_rows, core * column_half, column_half, axis=1)
-    own_half = lax.all_gather(own_half, "ep", axis=0, tiled=True)
+    own_half = jnp.concatenate(
+        lax.all_to_all(jnp.stack([own_half] * lax.axis_size("ep")), "ep", 0, 0), axis=0
+    )
     other_half = lax.ppermute(own_half, "ctx", [(i, i ^ 1) for i in range(ctx_count)])
     block_rows = out_proj.shape[0]
     attended_perm = (

time: 472 us -> 458 us (0.970)
  the two profiles are of different devices: /device:TPU:94 before, /device:TPU:96 now
where the time goes in v1:
time: 458 us; the launch traced here: 457 us
  blocking collectives  253 us (55%)
  waiting for transfers between devices  120 us (26%)
  local copies, waits for them, and re-layouts  31.8 us (7%)
  matrix products  24.7 us (5%)
  other arithmetic  19.1 us (4%)
  starting transfers between devices  7.22 us (2%)
    all_to_all x1, blocking collectives, shards(): lax.all_to_all(outgoing, 'ep', split_axis=0, concat_axis=0, tiled=True)  127 us
    all_to_all x1, waiting for transfers between devices, shards(): lax.all_to_all(replies, 'ep', split_axis=0, concat_axis=0, tiled=True)  120 us
    all_to_all x1, blocking collectives, shards(): lax.all_to_all(jnp.stack([own_half] * lax.axis_size('ep')), 'ep', 0, 0)  111 us
    all_gather x1, blocking collectives, shards(): column_rows = lax.all_gather(out_proj, 'ctx', axis=0, tiled=True)  14.6 us
    gather x1, local copies, waits for them, and re-layouts, shards(): returned.reshape(experts_all * capacity, model_width)[slot_ids]  12.2 us
    dot_general x1, matrix products, run_expert(): gate_up = jnp.dot(flat_in, weight_in, preferred_element_type=jnp.float32)  10.5 us
    scatter x1, local copies, waits for them, and re-layouts, shards(): outgoing = outgoing.at[slot_ids].set(jnp.repeat(normed, top_count, axis=0...  10.1 us
  transfers between devices with their start and end apart: 4, of which 1 were waited for; matrix products, arithmetic and copies ran while one was open for 5% of the time, Pallas kernels for 0%

profile of v1, /device:TPU:96, one launch (start us, length us, event | category | flops | bytes accessed | tf_op | source)
XLA Modules:
  0.0 457.3 jit_solution(1143000788525104983)
XLA Ops:
  0.6 0.0 copy-start
  0.7 14.6 %all_gather.3 = bf16[64,2048]{1,0:T(8,128)(2,1)S(1)} all-gather(bf16[8,2048]{1,0:T(8,128)(2,1)} %param.18), channel_id=1, replica_groups=mesh['ctx'=8,'ep'=32] {'ctx'}, dimensions={0}, use_global_device_ids=true | all-gather | bytes 294912 | tf_op jit(solution)/shard_map/all_gather | solution.py:91
  15.2 0.5 stack.11
  15.8 0.0 copy-start.8
  15.8 0.0 copy-start.9
  15.8 0.0 copy-start.11
  15.8 111.4 %all_to_all.15 = bf16[32,64,1024]{2,1,0:T(8,128)(2,1)} all-to-all(bf16[32,64,1024]{2,1,0:T(8,128)(2,1)S(1)} %stack.11), channel_id=1, replica_groups=mesh['ctx'=8,'ep'=32] {'ep'}, dimensions={0} | all-to-all | bytes 8388608 | tf_op jit(solution)/shard_map/all_to_all | solution.py:94
  127.2 0.0 collective-permute-start.2
  127.2 0.0 copy-done.8
  127.2 0.1 copy.21
  127.3 0.0 copy-done.9
  127.4 0.1 copy.22
  127.5 0.0 copy-start.10
  127.5 0.7 pad_maximum_fusion
  128.2 0.5 collective-permute-start
  128.7 0.0 copy-done.11
  128.7 0.1 copy.29
  128.8 0.1 eq.44
  128.9 9.0 %reduce-window.6 = s32[32,8,128]{2,1,0:T(8,128)S(1)} reduce-window(s32[32,8,128]{2,1,0:T(8,128)S(1)} %fusion.28, s32[]{:T(128)} %constant.73.clone.1), window={size=1x1x128 pad=0_0x0_0x127_0}, to_apply=%region_2.3 | reduce-window | flops 4161536 | bytes 262148 | tf_op jit(solution)/shard_map/reduce-window
  137.9 0.1 slice.28
  138.0 0.1 copy.31
  138.2 0.1 copy.32
  138.3 0.1 fusion.26
  138.4 0.1 broadcast_add_fusion
  138.5 0.1 eq.40
  138.6 0.1 copy.28
  138.7 0.1 mul.75
  138.9 0.0 collective-permute-done
  138.9 1.7 collective-permute-start.1
  140.6 2.0 copy.39
  142.6 2.3 copy.20
  144.9 1.0 constant_dynamic-update-slice_fusion.1
  145.9 0.0 collective-permute-done.1
  146.0 1.6 fusion.38
  147.6 0.0 copy-done.10
  147.6 0.3 fusion.11
  147.9 0.0 copy-done.6
  147.9 0.5 fusion.15
  148.5 0.0 copy-start.4
  148.5 0.1 copy.26
  148.6 0.7 copy-done.4
  149.3 0.1 broadcast_in_dim.14
  149.4 0.0 copy-start.7
  149.4 3.0 convolution_dynamic-update-slice_fusion.1
  152.4 0.0 copy-start.12
  152.4 0.0 collective-permute-done.2
  152.4 2.9 convolution_dynamic-update-slice_fusion
  155.4 0.1 add_convert_fusion
  155.5 0.0 copy-start.2
  155.5 0.2 fusion.16
  155.7 0.6 copy-done.2
  156.3 0.0 copy-done.12
  156.3 1.0 fusion.18
  157.3 10.1 %scatter_custom_fusion = bf16[1280,2048]{1,0:T(8,128)(2,1)} fusion(s32[1024]{0:T(1024)S(1)} %bitcast.103, bf16[]{:T(256)} %constant.86.clone.1, bf16[128,2048]{1,0:T(8,128)(2,1)} %fusion.18), kind=kCustom, calls=%fused_computation.7 | custom fusion | bytes 5767170 | tf_op jit(solution)/shard_map/scatter | solution.py:129
  167.3 127.4 %all_to_all.16 = bf16[32,40,2048]{2,1,0:T(8,128)(2,1)S(1)} all-to-all(bf16[32,40,2048]{2,1,0:T(8,128)(2,1)} %bitcast.86), channel_id=1, replica_groups=mesh['ctx'=8,'ep'=32] {'ep'}, dimensions={0} | all-to-all | bytes 10485760 | tf_op jit(solution)/shard_map/all_to_all | solution.py:136
  294.8 10.5 %fusion.1 = f32[1280,1536]{1,0:T(8,128)S(1)} fusion(bf16[1280,2048]{1,0:T(8,128)(2,1)S(1)} %bitcast.88, bf16[1,2048,1536]{2,1,0:T(8,128)(2,1)} %param.20), kind=kOutput, calls=%fused_computation.5 | convolution fusion | flops 8053063680 | bytes 19398656 | tf_op jit(solution)/shard_map/dot_general | solution.py:20
  305.3 6.1 %convolution_convert_fusion = bf16[1280,2048]{1,0:T(8,128)(2,1)} fusion(bf16[1,768,2048]{2,1,0:T(8,128)(2,1)S(1)} %copy-done, f32[1280,1536]{1,0:T(8,128)S(1)} %fusion.1), kind=kOutput, calls=%fused_computation.4 | convolution fusion | flops 4035051520 | bytes 16252928 | tf_op jit(solution)/shard_map/dot_general | solution.py:24
  311.4 5.0 %all-to-all-start.2 = ((bf16[32,40,2048]{2,1,0:T(8,128)(2,1)}), bf16[32,40,2048]{2,1,0:T(8,128)(2,1)}, u32[]{:S(2)}, u32[]{:S(2)}) async-start(bf16[32,40,2048]{2,1,0:T(8,128)(2,1)} %bitcast.87), calls=%async_computation.2 | async-start | bytes 10485760 | tf_op jit(solution)/shard_map/all_to_all | solution.py:141
  316.4 0.1 copy.27
  316.5 1.0 copy.33
  317.6 120.1 %all-to-all-done.2 = bf16[32,40,2048]{2,1,0:T(8,128)(2,1)} async-done(((bf16[32,40,2048]{2,1,0:T(8,128)(2,1)}), bf16[32,40,2048]{2,1,0:T(8,128)(2,1)}, u32[]{:S(2)}, u32[]{:S(2)}) %all-to-all-start.2) | async-done | bytes 5242912 | tf_op jit(solution)/shard_map/all_to_all | solution.py:141
  437.6 12.2 %gather_fusion = bf16[1024,2048]{1,0:T(8,128)(2,1)} fusion(bf16[1280,2048]{1,0:T(8,128)(2,1)} %bitcast.29, s32[1024]{0:T(1024)S(1)} %broadcast_clamp_fusion), kind=kCustom, calls=%fused_computation | custom fusion | bytes 8392704 | tf_op jit(solution)/shard_map/gather | solution.py:142
  449.8 6.6 %fusion = f32[128,2048]{1,0:T(8,128)S(1)} fusion(bf16[1024,2048]{1,0:T(8,128)(2,1)} %gather_fusion, f32[128,8]{1,0:T(8,128)S(1)} %copy.27), kind=kLoop, calls=%fused_computation.3 | loop fusion | flops 6029312 | bytes 5246976 | tf_op jit(solution)/shard_map/reduce_sum | solution.py:145
  456.4 0.9 fusion.19
  (26 shorter events, 0.2 us)
Async XLA Ops:
  0.6 304.7 %copy-start = (bf16[1,768,2048]{2,1,0:T(8,128)(2,1)S(1)}, bf16[1,768,2048]{2,1,0:T(8,128)(2,1)}, u32[]{:S(2)}) copy-start(bf16[1,768,2048]{2,1,0:T(8,128)(2,1)} %param.21) | copy-start | bytes 9437188
  15.8 111.4 %copy-start.8 = (bf16[128,256]{1,0:T(8,128)(2,1)S(1)}, bf16[128,256]{1,0:T(8,128)(2,1)}, u32[]{:S(2)}) copy-start(bf16[128,256]{1,0:T(8,128)(2,1)} %param.13) | copy-start | bytes 196612
  15.8 111.6 %copy-start.9 = (bf16[128,256]{1,0:T(8,128)(2,1)S(1)}, bf16[128,256]{1,0:T(8,128)(2,1)}, u32[]{:S(2)}) copy-start(bf16[128,256]{1,0:T(8,128)(2,1)} %param.14) | copy-start | bytes 196612
  15.8 112.9 %copy-start.11 = (s32[128,8]{0,1:T(8,128)S(1)}, s32[128,8]{0,1:T(8,128)}, u32[]{:S(2)}) copy-start(s32[128,8]{0,1:T(8,128)} %param.22) | copy-start | bytes 12292
  127.2 25.2 %collective-permute-start.2 = (bf16[2048,1024]{1,0:T(8,128)(2,1)}, bf16[2048,1024]{1,0:T(8,128)(2,1)}, u32[]{:S(2)}, u32[]{:S(2)}) collective-permute-start(bf16[2048,1024]{1,0:T(8,128)(2,1)} %bitcast.17), channel_id=1, source_target_pairs={{0,32},{32,0},{64,96},{96,64},{128,160},{160,128},{192,224},{224,1... | collective-permute-start | bytes 12582920 | tf_op jit(solution)/shard_map/ppermute | solution.py:96
  127.5 20.1 %copy-start.10 = (f32[128,16]{0,1:T(8,128)S(1)}, f32[128,16]{0,1:T(8,128)}, u32[]{:S(2)}) copy-start(f32[128,16]{0,1:T(8,128)} %param.16) | copy-start | bytes 24580
  128.2 10.7 %collective-permute-start = (bf16[2,128,256]{1,2,0:T(8,128)(2,1)}, bf16[2,128,256]{1,2,0:T(8,128)(2,1)}, u32[]{:S(2)}, u32[]{:S(2)}) collective-permute-start(bf16[2,128,256]{1,2,0:T(8,128)(2,1)} %pad_maximum_fusion), channel_id=1, source_target_pairs={{0,32},{32,64},{64,96},{96,128},{128,160},{160,192},{192,224},{224... | collective-permute-start | bytes 393224 | tf_op jit(solution)/shard_map/ppermute | solution.py:15
  138.9 7.0 %collective-permute-start.1 = (bf16[2,128,256]{1,2,0:T(8,128)(2,1)}, bf16[2,128,256]{1,2,0:T(8,128)(2,1)S(1)}, u32[]{:S(2)}, u32[]{:S(2)}) collective-permute-start(bf16[2,128,256]{1,2,0:T(8,128)(2,1)} %collective-permute-done), channel_id=1, source_target_pairs={{0,32},{32,64},{64,96},{96,128},{128,160},{160,192},{192,224},{224... | collective-permute-start | bytes 393224 | tf_op jit(solution)/shard_map/ppermute | solution.py:15
  144.9 3.0 copy-start.6
  148.5 0.8 copy-start.4
  149.4 6.0 %copy-start.7 = (bf16[128,2048]{1,0:T(8,128)(2,1)S(1)}, bf16[128,2048]{1,0:T(8,128)(2,1)}, u32[]{:S(2)}) copy-start(bf16[128,2048]{1,0:T(8,128)(2,1)} %param.17) | copy-start | bytes 1572868
  152.4 3.9 copy-start.12
  155.5 0.8 copy-start.2
  311.4 5.0 %copy-start.13 = (f32[128,8]{0,1:T(8,128)S(1)}, f32[128,8]{0,1:T(8,128)}, u32[]{:S(2)}) copy-start(f32[128,8]{0,1:T(8,128)} %param.23) | copy-start | bytes 12292
  311.4 5.1 %copy-start.5 = (bf16[128,2,8,128]{0,3,2,1:T(8,128)(2,1)S(1)}, bf16[128,2,8,128]{0,3,2,1:T(8,128)(2,1)}, u32[]{:S(2)}) copy-start(bf16[128,2,8,128]{0,3,2,1:T(8,128)(2,1)} %copy-done.4) | copy-start | bytes 1572868
  311.4 126.2 %all-to-all-start.2 = ((bf16[32,40,2048]{2,1,0:T(8,128)(2,1)}), bf16[32,40,2048]{2,1,0:T(8,128)(2,1)}, u32[]{:S(2)}, u32[]{:S(2)}) async-start(bf16[32,40,2048]{2,1,0:T(8,128)(2,1)} %bitcast.87), calls=%async_computation.2 | async-start | bytes 10485760 | tf_op jit(solution)/shard_map/all_to_all | solution.py:141
  437.6 19.7 %copy-start.1 = (bf16[1,768,2048]{2,1,0:T(8,128)(2,1)S(1)}, bf16[1,768,2048]{2,1,0:T(8,128)(2,1)}, u32[]{:S(2)}) copy-start(bf16[1,768,2048]{2,1,0:T(8,128)(2,1)} %param.21) | copy-start | bytes 9437188
  449.8 6.6 %copy-start.3 = (bf16[128,2048]{1,0:T(8,128)(2,1)S(1)}, bf16[128,2048]{1,0:T(8,128)(2,1)}, u32[]{:S(2)}) copy-start(bf16[128,2048]{1,0:T(8,128)(2,1)} %copy-done.2) | copy-start | bytes 1572868
